TPU v7x, 512 devices: a whole 4x4x16 slice. The times are simulated.
512 devices in a mesh: bond: 32 (over z_lo, x, core), leg: 16 (over z_hi, y).
Axes of the slice: x: 4, y: 4, z: 16 (z_hi: 4, z_lo: 4; z = z_hi * 4 + z_lo), core: 2. Of those that a mesh axis runs over, the one named last changes fastest.
Arguments:
- amplitudes: float32 [2, 1024, 262144], P(None, 'bond', 'leg'), may hold values from -6 to 6
- vectors: float32 [64, 262144], P(None, ('leg', 'bond')), may hold values from -0.01171875 to 0.01171875
- row_map: float32 [64, 4096], P('leg'), may hold values from -0.09375 to 0.09375
- col_map: float32 [64, 4096], P('bond'), may hold values from -0.09375 to 0.09375
Outputs:
- coarse: float32 [2, 8, 64, 64], P(None, None, 'leg', 'bond')
All inputs are finite; a program needn't handle non-finite values.
Results may differ from a plain program's by a relative error of at most 0.00014.
Values sent between devices are 32-bit elements; how exact they have to be, the bound alone decides.
A program may use at most 64 MiB of HBM per device.

v0:
```python
import jax
import jax.numpy as jnp
from jax import lax
from jax.sharding import PartitionSpec as P


def coarsen(slab, row_maps, col_maps):
    highest = lax.Precision.HIGHEST
    even = slab[:, 0::2]
    odd = slab[:, 1::2]
    inner = jnp.einsum("ztjc,qcd->ztqjd", even, col_maps, precision=highest)
    real_part = jnp.einsum("tqjd,tkd->tqjk", inner[0], odd[0], precision=highest) - jnp.einsum(
        "tqjd,tkd->tqjk", inner[1], odd[1], precision=highest
    )
    imag_part = jnp.einsum("tqjd,tkd->tqjk", inner[0], odd[1], precision=highest) + jnp.einsum(
        "tqjd,tkd->tqjk", inner[1], odd[0], precision=highest
    )
    paired = jnp.stack([real_part, imag_part])
    return jnp.einsum("pjk,ztqjk->ztpq", row_maps, paired, precision=highest)


def local(amplitudes, vectors, row_map, col_map):
    highest = lax.Precision.HIGHEST
    bond_dim = vectors.shape[0]
    partial_proj = jnp.einsum(
        "jk,zrk->zjr",
        lax.all_gather(vectors, "bond", axis=1, tiled=True),
        amplitudes,
        precision=highest,
    )
    summed = lax.psum(partial_proj, "leg")
    projected = lax.all_gather(summed, "bond", axis=2, tiled=True)
    slab_count = projected.shape[2] // bond_dim
    slab = projected.reshape(2, bond_dim, slab_count, bond_dim).transpose(0, 2, 1, 3)
    row_maps = row_map.reshape(row_map.shape[0], bond_dim, bond_dim)
    col_maps = col_map.reshape(col_map.shape[0], bond_dim, bond_dim)
    return coarsen(slab, row_maps, col_maps)


def solution(mesh):
    return jax.shard_map(
        local,
        mesh=mesh,
        in_specs=(
            P(None, "bond", "leg"),
            P(None, ("leg", "bond")),
            P("leg", None),
            P("bond", None),
        ),
        out_specs=P(None, None, "leg", "bond"),
        check_vma=False,
    )
```

profile of v0, /device:TPU:1, one launch (start us, length us, event | category | flops | bytes accessed | tf_op | source)
XLA Modules:
  0.0 250.0 jit_solution(4915478160259681730)
XLA Ops:
  6.5 0.0 all-gather.2.cloned.1.call-start
  6.5 0.7 all-gather.2.cloned.1.call-update
  7.3 0.9 reshape.14
  8.1 1.0 reshape.11
  9.1 73.8 %all-gather.2.cloned.1.call-done = f32[64,16384]{1,0:T(8,128)} async-done(((f32[64,512]{1,0:T(8,128)}), f32[64,16384]{1,0:T(8,128)}) %all-gather.2.cloned.1.call-update) | async-done | bytes 4194320 | tf_op jit(solution)/shard_map/all_gather | solution.py:27
  82.8 6.9 %fusion.4 = f32[2,64,32]{1,2,0:T(8,128)S(1)} fusion(f32[2,32,16384]{2,1,0:T(8,128)} %param.4, f32[64,16384]{1,0:T(8,128)} %all-gather.2.cloned.1.call-done), kind=kOutput, calls=%fused_computation.7 | convolution fusion | flops 805306368 | bytes 8404992 | tf_op jit(solution)/shard_map/jk,zrk->zjr/dot_general | solution.py:25
  89.8 84.2 %psum.7 = f32[2,64,32]{1,2,0:T(8,128)S(1)} all-reduce(f32[2,64,32]{1,2,0:T(8,128)S(1)} %fusion.4), channel_id=1, replica_groups=mesh['bond'=32,'leg'=16] {'leg'}, use_global_device_ids=true, to_apply=%region_0.0 | all-reduce | flops 4096 | bytes 32768 | tf_op jit(solution)/shard_map/psum | solution.py:31
  174.0 57.6 %all_gather.7 = f32[2,64,1024]{1,2,0:T(8,128)S(1)} all-gather(f32[2,64,32]{1,2,0:T(8,128)S(1)} %psum.7), channel_id=1, replica_groups=mesh['bond'=32,'leg'=16] {'bond'}, dimensions={2}, use_global_device_ids=true | all-gather | bytes 540672 | tf_op jit(solution)/shard_map/all_gather | solution.py:32
  231.5 0.3 copy.5
  231.9 1.0 convolution_bitcast_fusion
  232.9 0.6 fusion.10
  233.5 0.6 fusion.11
  234.1 0.6 fusion.2
  234.8 0.6 fusion.3
  235.4 0.1 pad_maximum_fusion
  235.5 7.0 %convolution_bitcast_fusion.1 = f32[2,8,4,2]{1,2,3,0:T(4,128)S(1)} fusion(f32[2,8,2,64,64]{4,3,2,1,0:T(8,128)S(1)} %pad_maximum_fusion, f32[4,64,64,1,1]{2,1,0,4,3:T(8,128)S(1)} %bitcast.55), kind=kOutput, calls=%fused_computation.8 | convolution fusion | flops 6291456 | bytes 590336 | tf_op jit(solution)/shard_map/pjk,ztqjk->ztpq/dot_general | solution.py:19
  242.5 0.6 copy.8
  (1 shorter events, 0.0 us)
Async XLA Ops:
  6.5 76.3 %all-gather.2.cloned.1.call-start = ((), (), s32[]{:S(2)}) async-start(), calls=%async_computation | async-start | bytes 4325376 | tf_op jit(solution)/shard_map/all_gather | solution.py:27
Sparse Core Ops, SparseCore 0:
  9.5 73.3 all-gather.1
where the time goes:
time: 250 us
  blocking collectives  142 us (57%)
  waiting for transfers between devices  74.5 us (30%)
  matrix products  17.4 us (7%)
  between operations  13.5 us (5%)
  local copies, waits for them, and re-layouts  2.82 us (1%)
    psum x1, blocking collectives, local(): summed = lax.psum(partial_proj, 'leg')  84.2 us
    all_gather x1, waiting for transfers between devices, local(): lax.all_gather(vectors, 'bond', axis=1, tiled=True)  73.8 us
    all_gather x1, blocking collectives, local(): projected = lax.all_gather(summed, 'bond', axis=2, tiled=True)  57.6 us
    dot_general x1, matrix products, coarsen(): return jnp.einsum('pjk,ztqjk->ztpq', row_maps, paired, precision=highest)  6.99 us
    dot_general x1, matrix products, local(): jnp.einsum('jk,zrk->zjr', lax.all_gather(vectors, 'bond', axis=1, tiled=T...  6.94 us
  transfers between devices with their start and end apart: 1, of which 1 were waited for; matrix products, arithmetic and copies ran while one was open for 1% of the time, Pallas kernels for 0%

commit v1 on v0

v1 whole, which is shorter than its diff:
```python
import functools

import jax
import jax.numpy as jnp
from jax import lax
from jax.experimental import pallas as pl
from jax.experimental.pallas import tpu as pltpu
from jax.sharding import PartitionSpec as P

MESH = pl.DeviceIdType.MESH
F32, BF16 = jnp.float32, jnp.bfloat16
NT = (((1,), (1,)), ((), ()))
NN = (((1,), (0,)), ((), ()))


def halves(v):
    hi = v.astype(BF16)
    return hi, (v - hi.astype(F32)).astype(BF16)


def kernel(
    amp, vec, rmap, cmap, out,
    abuf, vbuf, rbuf, cbuf, acc, part, piece8, piece4, slabs, rwide, rcat, ccat, bcat, gbuf, hbuf, msg, res,
    a_in, a_rin, a_rout, v_in, z_in, x_in, v_out, map_in, c_in, c_out,
    p8_in, p8_out, p4_in, p4_out, s_in, s_out, m_in, m_out,
):
    bond, leg = lax.axis_index("bond"), lax.axis_index("leg")
    core, x, zl = lax.rem(bond, 2), lax.rem(bond // 2, 4), bond // 8
    y, zh = lax.rem(leg, 4), leg // 4

    def dev(x_=x, zl_=zl, core_=core, y_=y, zh_=zh):
        return ((zl_ * 4 + x_) * 2 + core_, zh_ * 4 + y_)

    def rot(v, d):
        return lax.rem(v + (d + 4), 4)

    def remote(src, dst, send, recv, device):
        return pltpu.make_async_remote_copy(
            src_ref=src, dst_ref=dst, send_sem=send, recv_sem=recv, device_id=device, device_id_type=MESH
        )

    def drain(ref, sem):
        pltpu.make_async_copy(ref, ref, sem).wait()

    barrier = pltpu.get_barrier_semaphore()

    def greet(device):
        pl.semaphore_signal(barrier, inc=1, device_id=device, device_id_type=MESH)

    def row_peer(k):
        flat = lax.rem(((x * 4 + y) * 2 + core) + k, 32)
        return flat // 8, lax.rem(flat // 2, 4), lax.rem(flat, 2)

    @pl.loop(1, 32)
    def _(k):
        x_, y_, core_ = row_peer(k)
        greet(dev(x_=x_, y_=y_, core_=core_))

    for d in (1, 2, 3):
        greet(dev(zl_=rot(zl, d)))
        greet(dev(zh_=rot(zh, d)))

    own = zl * 4 + x
    pltpu.make_async_copy(vec, vbuf.at[own], v_in).start()
    map_copies = (pltpu.make_async_copy(rmap, rbuf, map_in.at[0]), pltpu.make_async_copy(cmap, cbuf.at[zl], map_in.at[1]))
    for copy in map_copies:
        copy.start()

    def block_of(i, xo):
        return rot(zl, -i) * 4 + rot(x, xo)

    def a_local(n):
        cols = pl.ds(pl.multiple_of((n * 2 + core) * 512, 512), 512)
        return pltpu.make_async_copy(amp.at[:, cols], abuf.at[core, n], a_in.at[n])

    def a_remote(n):
        cols = pl.ds(pl.multiple_of((n * 2 + 1 - core) * 512, 512), 512)
        return remote(amp.at[:, cols], abuf.at[core, n], a_rout, a_rin.at[n], dev(core_=1 - core))

    pl.semaphore_wait(barrier, 37)

    def x_send(i, k):
        half, way = ((0, 1), (1, -1), (1, 1), (0, -1))[k]
        n, rows = block_of(i, 0), pl.ds(half * 32, 32)
        src = vbuf.at[n, rows]
        return remote(src, vbuf.at[n, rows], v_out, x_in.at[i, k], dev(x_=rot(x, way)))

    def x_relay(i, k):
        half, way = ((0, 1), (1, -1))[k]
        n, rows = block_of(i, -way), pl.ds(half * 32, 32)
        return remote(vbuf.at[n, rows], vbuf.at[n, rows], v_out, x_in.at[i, 4 + k], dev(x_=rot(x, way)))

    z_sends = [
        remote(vec, vbuf.at[own], v_out, z_in.at[d - 1], dev(zl_=rot(zl, d))) for d in (1, 2, 3)
    ]
    for half, way, k in ((0, 1, 0), (1, -1, 1)):
        rows = pl.ds(half * 32, 32)
        remote(vec.at[rows], vbuf.at[own, rows], v_out, x_in.at[0, k], dev(x_=rot(x, way))).start()
    z_sends[0].start()
    for half, way, k in ((1, 1, 2), (0, -1, 3)):
        rows = pl.ds(half * 32, 32)
        remote(vec.at[rows], vbuf.at[own, rows], v_out, x_in.at[0, k], dev(x_=rot(x, way))).start()
    z_sends[1].start()
    z_sends[2].start()

    @pl.loop(0, 16)
    def _(m):
        n = block_of(m // 4, lax.rem(m, 4))
        a_local(n).start()
        a_remote(n).start()

    acc[...] = jnp.zeros_like(acc)

    def project(n):
        a_local(n).wait()
        a_remote(n).wait_recv()
        a_hi, a_lo = halves(abuf[:, n].reshape(128, 512))
        v_hi, v_lo = halves(vbuf[n])
        acc[...] += lax.dot_general(
            jnp.concatenate([a_hi, a_lo], 0), jnp.concatenate([v_hi, v_lo], 0), NT, preferred_element_type=F32
        )

    def relay(i):
        for k in (0, 1):
            x_send(i, k).wait_recv()
            x_relay(i, k).start()

    def far(i):
        for k in (0, 1):
            x_relay(i, k).wait_recv()
        project(block_of(i, 2))

    for copy in map_copies:
        copy.wait()
    c_sends = [
        remote(cbuf.at[zl], cbuf.at[zl], c_out, c_in.at[d - 1], dev(zl_=rot(zl, d))) for d in (1, 2, 3)
    ]
    for copy in c_sends:
        copy.start()
    relay(0)

    def maps():
        first = lax.broadcasted_iota(jnp.int32, (32, 128), 1) < 64
        for p in range(4):
            v = rbuf[:, p, :]
            swapped = pltpu.roll(v, 64, 1)
            for par in range(2):
                low, high = (v, swapped) if par == 0 else (swapped, v)
                rwide[p, pl.ds(par, 32, stride=2)] = jnp.where(first, low, 0.0)
                rwide[p, pl.ds(64 + par, 32, stride=2)] = jnp.where(first, 0.0, high)
            hi, lo = halves(rwide[p])
            for k, w in enumerate((hi, hi, lo)):
                rcat[k * 128 : k * 128 + 128, p * 128 : p * 128 + 128] = w
        bcat[...] = jnp.zeros_like(bcat)
        for d in (1, 2, 3):
            c_sends[d - 1].wait_recv()
        for k in range(4):
            for q in range(2):
                hi, lo = halves(cbuf[k, :, q, :])
                ccat[k * 64 + q * 32 : k * 64 + q * 32 + 32] = jnp.concatenate([hi, lo, hi], 1)

    @pl.loop(0, 4)
    def _(i):
        @pl.when(i < 3)
        def _():
            remote(vec, vbuf.at[own], v_out, z_in.at[i], dev()).wait_recv()
            for k in range(4):
                x_send(i + 1, k).start()

        @pl.when(i > 0)
        def _():
            relay(i)

        @pl.when(i == 0)
        def _():
            pltpu.make_async_copy(vec, vbuf.at[own], v_in).wait()

        project(block_of(i, 0))

        @pl.when(i > 0)
        def _():
            far(i - 1)

        x_send(i, 2).wait_recv()
        project(block_of(i, -1))
        x_send(i, 3).wait_recv()
        project(block_of(i, 1))

        @pl.when(i == 0)
        def _():
            maps()

    far(3)

    both = acc[:128] + acc[128:]
    both = both + pltpu.roll(both, 64, 1)
    first = lax.broadcasted_iota(jnp.int32, (32, 128), 1) < 64
    for s in range(2):
        part[s * 32 : s * 32 + 32] = jnp.where(first, both[s * 64 : s * 64 + 32], both[s * 64 + 32 : s * 64 + 64])

    mine = y * 2 + core

    def eighth(k):
        return pl.ds(pl.multiple_of(k * 8, 8), 8)

    def scatter(k):
        to = lax.rem(mine + k, 8)
        return remote(part.at[eighth(to)], piece8.at[mine], p8_out, p8_in.at[k - 1], dev(y_=to // 2, core_=lax.rem(to, 2)))

    for k in range(1, 8):
        scatter(k).start()
    piece8[mine] = part[eighth(mine)]
    for k in range(1, 8):
        scatter(k).wait_recv()
    piece4[zh] = jnp.sum(piece8[...], axis=0)

    def spread(d):
        return remote(piece4.at[zh], piece4.at[zh], p4_out, p4_in.at[d - 1], dev(zh_=rot(zh, d)))

    for d in (2, 1, 3):
        spread(d).start()
    for d in (1, 2, 3):
        spread(d).wait_recv()
    here = pl.ds(pl.multiple_of(x * 64 + mine * 8, 8), 8)
    slabs[here] = jnp.sum(piece4[...], axis=0)

    @pl.loop(1, 32)
    def _(k):
        x_, y_, core_ = row_peer(k)
        remote(slabs.at[here], slabs.at[here], s_out, s_in, dev(x_=x_, y_=y_, core_=core_)).start()

    drain(slabs.at[pl.ds(0, 248)], s_in)

    lhs = jnp.concatenate(
        [slabs[pl.ds(t * 128 + par, 32, stride=2)] for t in range(2) for par in range(2)], 0
    )
    l_hi, l_lo = halves(lhs)
    gbuf[...] = lax.dot_general(
        jnp.concatenate([l_hi, l_lo, l_hi], 1), rcat[...], NN, preferred_element_type=F32
    )
    for t in range(2):
        b_hi, b_lo = halves(slabs[t * 128 + 64 : t * 128 + 128])
        for k, v in enumerate((b_hi, b_hi, b_lo)):
            for par in range(2):
                bcat[t, k * 128 + par * 64 : k * 128 + par * 64 + 64, par * 128 : par * 128 + 128] = v
        hbuf[t] = lax.dot_general(ccat[...], bcat[t], NN, preferred_element_type=F32)

    @pl.loop(0, 4)
    def _(to):
        for t in range(2):
            sums = [[None] * 2 for _ in range(8)]
            for q in range(2):
                rows = pl.ds(pl.multiple_of(to * 64 + q * 32, 32), 32)
                h = [hbuf[t, rows, par * 128 : par * 128 + 128] for par in range(2)]
                for p in range(4):
                    g = [gbuf[t * 64 + par * 32 : t * 64 + par * 32 + 32, p * 128 : p * 128 + 128] for par in range(2)]
                    straight = g[0] * h[0] + g[1] * h[1]
                    crossed = pltpu.roll(g[0], 64, 1) * h[0] + pltpu.roll(g[1], 64, 1) * h[1]
                    sums[p][q] = jnp.sum(straight, axis=0, keepdims=True)
                    sums[4 + p][q] = jnp.sum(crossed, axis=0, keepdims=True)
            msg[to, t] = jnp.concatenate([v for pair in sums for v in pair], 0)

    def answer(d):
        return remote(msg.at[rot(zl, d)], res.at[zl], m_out, m_in.at[d - 1], dev(zl_=rot(zl, d)))

    for d in (1, 2, 3):
        answer(d).start()
    res[zl] = msg[zl]
    for d in (1, 2, 3):
        answer(d).wait_recv()
    row = lax.broadcasted_iota(jnp.int32, (16, 128), 0)
    lane = lax.broadcasted_iota(jnp.int32, (16, 128), 1)
    minus = jnp.logical_and(row < 8, lane >= 64)
    total = jnp.zeros((16, 128), F32)
    for k in range(8):
        v = res[k // 2, k % 2]
        total = total + jnp.where(lane == k, jnp.sum(jnp.where(minus, -v, v), axis=1, keepdims=True), 0.0)
    out[...] = total[:, :8]

    drain(vbuf.at[pl.ds(0, 15)], v_out)
    drain(abuf.at[0], a_rout)
    drain(cbuf.at[pl.ds(0, 3)], c_out)
    drain(piece8.at[pl.ds(0, 7)], p8_out)
    drain(piece4.at[pl.ds(0, 3)], p4_out)
    drain(slabs.at[pl.ds(0, 248)], s_out)
    drain(res.at[pl.ds(0, 3)], m_out)


def local(amplitudes, vectors, row_map, col_map):
    dma = pltpu.SemaphoreType.DMA
    got = pl.pallas_call(
        kernel,
        out_shape=jax.ShapeDtypeStruct((16, 8), F32),
        in_specs=[pl.BlockSpec(memory_space=pl.ANY)] * 4,
        out_specs=pl.BlockSpec(memory_space=pltpu.VMEM),
        scratch_shapes=[
            pltpu.VMEM((2, 16, 64, 512), F32),
            pltpu.VMEM((16, 64, 512), F32),
            pltpu.VMEM((32, 4, 128), F32),
            pltpu.VMEM((4, 32, 2, 128), F32),
            pltpu.VMEM((256, 128), F32),
            pltpu.VMEM((64, 128), F32),
            pltpu.VMEM((8, 8, 128), F32),
            pltpu.VMEM((4, 8, 128), F32),
            pltpu.VMEM((256, 128), F32),
            pltpu.VMEM((4, 128, 128), F32),
            pltpu.VMEM((384, 512), BF16),
            pltpu.VMEM((256, 384), BF16),
            pltpu.VMEM((2, 384, 256), BF16),
            pltpu.VMEM((128, 512), F32),
            pltpu.VMEM((2, 256, 256), F32),
            pltpu.VMEM((4, 2, 16, 128), F32),
            pltpu.VMEM((4, 2, 16, 128), F32),
            dma((16,)), dma((16,)), dma, dma, dma((3,)), dma((4, 6)), dma, dma((2,)), dma((3,)), dma,
            dma((7,)), dma, dma((3,)), dma, dma, dma, dma((3,)), dma,
        ],
        compiler_params=pltpu.CompilerParams(collective_id=0, has_side_effects=True),
    )(
        amplitudes.reshape(64, -1),
        vectors,
        row_map.reshape(4, 32, 128).transpose(1, 0, 2),
        col_map.reshape(2, 32, 128).transpose(1, 0, 2),
    )
    return got.reshape(2, 4, 2, 8).transpose(0, 3, 1, 2)


def solution(mesh):
    return jax.shard_map(
        local,
        mesh=mesh,
        in_specs=(
            P(None, "bond", "leg"),
            P(None, ("leg", "bond")),
            P("leg", None),
            P("bond", None),
        ),
        out_specs=P(None, None, "leg", "bond"),
        check_vma=False,
    )
```

time: 250 us -> 68 us (0.27)
  blocking collectives: 142 us -> 0 us
  waiting for transfers between devices: 74.5 us -> 0 us
  Pallas kernels: 0 us -> 66.6 us
  matrix products: 17.4 us -> 0 us
  between operations: 13.5 us -> 0.01 us
    psum x1 -> x0, blocking collectives: 84.2 us -> none  [local(): summed = lax.psum(partial_proj, 'leg')]
    all_gather x1 -> x0, waiting for transfers between devices: 73.8 us -> none  [local(): lax.all_gather(vectors, 'bond', axis=1, tiled=True)]
    pallas_call x0 -> x1, Pallas kernels: none -> 66.6 us  [local(): pl.pallas_call(kernel, out_shape=jax.ShapeDtypeStruct((16, 8), F32), in_s...]
    all_gather x1 -> x0, blocking collectives: 57.6 us -> none  [local(): projected = lax.all_gather(summed, 'bond', axis=2, tiled=True)]
    dot_general x7 -> x0, matrix products: 17.4 us -> none  [the longest x1 6.99 us: coarsen(): return jnp.einsum('pjk,ztqjk->ztpq', row_maps, paired, precision=highest)]
  transfers between devices with their start and end apart: 1 -> 0, of which waited for: 1 -> 0; matrix products, arithmetic and copies ran while one was open for 1% -> 0% of each run, Pallas kernels for 0% -> 0%
where the time goes in v1:
time: 68 us; the launch traced here: 67.9 us
  Pallas kernels  66.6 us (98%)
  local copies, waits for them, and re-layouts  1.3 us (2%)
    pallas_call x1, Pallas kernels, local(): pl.pallas_call(kernel, out_shape=jax.ShapeDtypeStruct((16, 8), F32), in_s...  66.6 us

profile of v1, /device:TPU:1, one launch (start us, length us, event | category | flops | bytes accessed | tf_op | source)
XLA Modules:
  0.0 67.9 jit_solution(225814091676088756)
XLA Ops:
  0.0 66.6 %shard_map.46 = f32[16,8]{1,0:T(8,128)} custom-call(f32[64,16384]{1,0:T(8,128)} %bitcast.10, f32[64,512]{1,0:T(8,128)} %vec.1, f32[32,4,128]{2,1,0:T(4,128)} %bitcast.11, f32[32,2,128]{2,1,0:T(2,128)} %bitcast.12), custom_call_target="tpu_custom_call" | custom-call | tf_op jit(solution)/shard_map/pallas_call | solution.py:291
  66.6 1.3 %copy.6 = f32[2,8,4,2]{1,3,2,0:T(2,128)} copy(f32[2,8,4,2]{1,3,2,0:T(2,128)} %bitcast.13) | data formatting | bytes 1024

commit v2 on v1

--- a/solution.py
+++ b/solution.py
@@ -22,7 +22,7 @@
     amp, vec, rmap, cmap, out,
     abuf, vbuf, rbuf, cbuf, acc, part, piece8, piece4, slabs, rwide, rcat, ccat, bcat, gbuf, hbuf, msg, res,
     a_in, a_rin, a_rout, v_in, z_in, x_in, v_out, map_in, c_in, c_out,
-    p8_in, p8_out, p4_in, p4_out, s_in, s_out, m_in, m_out,
+    p8_in, p8_out, p4_in, p4_out, s_in, s_out, m_in, m_out, word,
 ):
     bond, leg = lax.axis_index("bond"), lax.axis_index("leg")
     core, x, zl = lax.rem(bond, 2), lax.rem(bond // 2, 4), bond // 8
@@ -42,23 +42,20 @@
     def drain(ref, sem):
         pltpu.make_async_copy(ref, ref, sem).wait()
 
+    def up(d):
+        z_ = lax.rem(zh * 4 + zl + (d + 16), 16)
+        return dev(zl_=lax.rem(z_, 4), zh_=z_ // 4)
+
+    beside = [dev(x_=rot(x, d)) for d in (1, -1)] + [dev(y_=rot(y, d)) for d in (1, -1)] + [up(1), up(-1)]
+    partner = dev(core_=1 - core)
+    rounds = (beside, [partner, up(2), up(-2)], [dev(y_=rot(y, d)) for d in (1, 2, 3)] + [up(4), up(-4)])
+
+    def tell(sem, devices):
+        for device in devices:
+            pl.semaphore_signal(sem, inc=1, device_id=device, device_id_type=MESH)
+
     barrier = pltpu.get_barrier_semaphore()
-
-    def greet(device):
-        pl.semaphore_signal(barrier, inc=1, device_id=device, device_id_type=MESH)
-
-    def row_peer(k):
-        flat = lax.rem(((x * 4 + y) * 2 + core) + k, 32)
-        return flat // 8, lax.rem(flat // 2, 4), lax.rem(flat, 2)
-
-    @pl.loop(1, 32)
-    def _(k):
-        x_, y_, core_ = row_peer(k)
-        greet(dev(x_=x_, y_=y_, core_=core_))
-
-    for d in (1, 2, 3):
-        greet(dev(zl_=rot(zl, d)))
-        greet(dev(zh_=rot(zh, d)))
+    tell(barrier, beside + [partner])
 
     own = zl * 4 + x
     pltpu.make_async_copy(vec, vbuf.at[own], v_in).start()
@@ -66,8 +63,15 @@
     for copy in map_copies:
         copy.start()
 
+    def row_of(i):
+        low, odd = zl < 2, lax.rem(zl, 2) == 1
+        first = jnp.where(odd, 2, 1)
+        second = jnp.where(odd, jnp.where(low, 0, 1), jnp.where(low, 2, 3))
+        third = jnp.where(low, 3, 0)
+        return jnp.where(i == 0, zl, jnp.where(i == 1, first, jnp.where(i == 2, second, third)))
+
     def block_of(i, xo):
-        return rot(zl, -i) * 4 + rot(x, xo)
+        return row_of(i) * 4 + rot(x, xo)
 
     def a_local(n):
         cols = pl.ds(pl.multiple_of((n * 2 + core) * 512, 512), 512)
@@ -77,7 +81,8 @@
         cols = pl.ds(pl.multiple_of((n * 2 + 1 - core) * 512, 512), 512)
         return remote(amp.at[:, cols], abuf.at[core, n], a_rout, a_rin.at[n], dev(core_=1 - core))
 
-    pl.semaphore_wait(barrier, 37)
+    pl.semaphore_wait(barrier, 7)
+    tell(word.at[0], rounds[0])
 
     def x_send(i, k):
         half, way = ((0, 1), (1, -1), (1, 1), (0, -1))[k]
@@ -90,24 +95,43 @@
         n, rows = block_of(i, -way), pl.ds(half * 32, 32)
         return remote(vbuf.at[n, rows], vbuf.at[n, rows], v_out, x_in.at[i, 4 + k], dev(x_=rot(x, way)))
 
-    z_sends = [
-        remote(vec, vbuf.at[own], v_out, z_in.at[d - 1], dev(zl_=rot(zl, d))) for d in (1, 2, 3)
-    ]
-    for half, way, k in ((0, 1, 0), (1, -1, 1)):
+    middle = jnp.logical_and(zl > 0, zl < 3)
+
+    def z_send(i):
+        return remote(vec, vbuf.at[own], v_out, z_in.at[zl], dev(zl_=row_of(i)))
+
+    def z_take(i):
+        r = row_of(i)
+        n = r * 4 + x
+        remote(vec, vbuf.at[n], v_out, z_in.at[r], dev()).wait_recv()
+
+        @pl.when(middle)
+        def _():
+            to = jnp.where(r > zl, zl - 1, zl + 1)
+            remote(vbuf.at[n], vbuf.at[n], v_out, z_in.at[r], dev(zl_=to)).start()
+
+    for half, way, k in ((0, 1, 0), (1, -1, 1), (1, 1, 2), (0, -1, 3)):
         rows = pl.ds(half * 32, 32)
         remote(vec.at[rows], vbuf.at[own, rows], v_out, x_in.at[0, k], dev(x_=rot(x, way))).start()
-    z_sends[0].start()
-    for half, way, k in ((1, 1, 2), (0, -1, 3)):
-        rows = pl.ds(half * 32, 32)
-        remote(vec.at[rows], vbuf.at[own, rows], v_out, x_in.at[0, k], dev(x_=rot(x, way))).start()
-    z_sends[1].start()
-    z_sends[2].start()
-
-    @pl.loop(0, 16)
+        if k == 1:
+            z_send(1).start()
+
+            @pl.when(middle)
+            def _():
+                z_send(2).start()
+    for m in range(4):
+        a_local(block_of(0, m)).start()
+        a_remote(block_of(0, m)).start()
+    pl.semaphore_wait(word.at[0], 6)
+    tell(word.at[1], rounds[1])
+    @pl.loop(4, 16)
     def _(m):
         n = block_of(m // 4, lax.rem(m, 4))
         a_local(n).start()
         a_remote(n).start()
+
+    pl.semaphore_wait(word.at[1], 3)
+    tell(word.at[2], rounds[2])
 
     acc[...] = jnp.zeros_like(acc)
 
@@ -130,14 +154,12 @@
             x_relay(i, k).wait_recv()
         project(block_of(i, 2))
 
+    relay(0)
     for copy in map_copies:
         copy.wait()
     c_sends = [
         remote(cbuf.at[zl], cbuf.at[zl], c_out, c_in.at[d - 1], dev(zl_=rot(zl, d))) for d in (1, 2, 3)
     ]
-    for copy in c_sends:
-        copy.start()
-    relay(0)
 
     def maps():
         first = lax.broadcasted_iota(jnp.int32, (32, 128), 1) < 64
@@ -163,9 +185,21 @@
     def _(i):
         @pl.when(i < 3)
         def _():
-            remote(vec, vbuf.at[own], v_out, z_in.at[i], dev()).wait_recv()
+            @pl.when(jnp.logical_or(i == 0, jnp.logical_not(middle)))
+            def _():
+                z_take(i + 1)
+
             for k in range(4):
                 x_send(i + 1, k).start()
+
+        @pl.when(jnp.logical_and(i < 2, middle))
+        def _():
+            z_take(i + 2)
+
+        @pl.when(i == 2)
+        def _():
+            for copy in c_sends:
+                copy.start()
 
         @pl.when(i > 0)
         def _():
@@ -185,10 +219,6 @@
         project(block_of(i, -1))
         x_send(i, 3).wait_recv()
         project(block_of(i, 1))
-
-        @pl.when(i == 0)
-        def _():
-            maps()
 
     far(3)
 
@@ -198,6 +228,7 @@
     for s in range(2):
         part[s * 32 : s * 32 + 32] = jnp.where(first, both[s * 64 : s * 64 + 32], both[s * 64 + 32 : s * 64 + 64])
 
+    pl.semaphore_wait(word.at[2], 5)
     mine = y * 2 + core
 
     def eighth(k):
@@ -207,7 +238,7 @@
         to = lax.rem(mine + k, 8)
         return remote(part.at[eighth(to)], piece8.at[mine], p8_out, p8_in.at[k - 1], dev(y_=to // 2, core_=lax.rem(to, 2)))
 
-    for k in range(1, 8):
+    for k in (5, 4, 3, 2, 6, 7, 1):
         scatter(k).start()
     piece8[mine] = part[eighth(mine)]
     for k in range(1, 8):
@@ -219,15 +250,18 @@
 
     for d in (2, 1, 3):
         spread(d).start()
+    maps()
     for d in (1, 2, 3):
         spread(d).wait_recv()
     here = pl.ds(pl.multiple_of(x * 64 + mine * 8, 8), 8)
     slabs[here] = jnp.sum(piece4[...], axis=0)
 
-    @pl.loop(1, 32)
-    def _(k):
-        x_, y_, core_ = row_peer(k)
-        remote(slabs.at[here], slabs.at[here], s_out, s_in, dev(x_=x_, y_=y_, core_=core_)).start()
+    for dx in (2, 1, 3, 0):
+        for dy in (2, 1, 3, 0):
+            for core_ in (1 - core, core):
+                if dx or dy or core_ is not core:
+                    to = dev(x_=rot(x, dx), y_=rot(y, dy), core_=core_)
+                    remote(slabs.at[here], slabs.at[here], s_out, s_in, to).start()
 
     drain(slabs.at[pl.ds(0, 248)], s_in)
 
@@ -245,8 +279,13 @@
                 bcat[t, k * 128 + par * 64 : k * 128 + par * 64 + 64, par * 128 : par * 128 + 128] = v
         hbuf[t] = lax.dot_general(ccat[...], bcat[t], NN, preferred_element_type=F32)
 
+    row = lax.broadcasted_iota(jnp.int32, (16, 128), 0)
+    lane = lax.broadcasted_iota(jnp.int32, (16, 128), 1)
+    minus = jnp.logical_and(row < 8, lane >= 64)
+
     @pl.loop(0, 4)
     def _(to):
+        total = jnp.zeros((16, 128), F32)
         for t in range(2):
             sums = [[None] * 2 for _ in range(8)]
             for q in range(2):
@@ -258,7 +297,10 @@
                     crossed = pltpu.roll(g[0], 64, 1) * h[0] + pltpu.roll(g[1], 64, 1) * h[1]
                     sums[p][q] = jnp.sum(straight, axis=0, keepdims=True)
                     sums[4 + p][q] = jnp.sum(crossed, axis=0, keepdims=True)
-            msg[to, t] = jnp.concatenate([v for pair in sums for v in pair], 0)
+            v = jnp.concatenate([v for pair in sums for v in pair], 0)
+            v = jnp.sum(jnp.where(minus, -v, v), axis=1, keepdims=True)
+            total = total + jnp.where(lane == zl * 2 + t, v, 0.0)
+        msg[to] = total
 
     def answer(d):
         return remote(msg.at[rot(zl, d)], res.at[zl], m_out, m_in.at[d - 1], dev(zl_=rot(zl, d)))
@@ -268,16 +310,14 @@
     res[zl] = msg[zl]
     for d in (1, 2, 3):
         answer(d).wait_recv()
-    row = lax.broadcasted_iota(jnp.int32, (16, 128), 0)
-    lane = lax.broadcasted_iota(jnp.int32, (16, 128), 1)
-    minus = jnp.logical_and(row < 8, lane >= 64)
-    total = jnp.zeros((16, 128), F32)
-    for k in range(8):
-        v = res[k // 2, k % 2]
-        total = total + jnp.where(lane == k, jnp.sum(jnp.where(minus, -v, v), axis=1, keepdims=True), 0.0)
-    out[...] = total[:, :8]
-
-    drain(vbuf.at[pl.ds(0, 15)], v_out)
+    out[...] = jnp.sum(res[...], axis=0)[:, :8]
+
+    drain(vbuf.at[pl.ds(0, 13)], v_out)
+
+    @pl.when(middle)
+    def _():
+        drain(vbuf.at[pl.ds(0, 4)], v_out)
+
     drain(abuf.at[0], a_rout)
     drain(cbuf.at[pl.ds(0, 3)], c_out)
     drain(piece8.at[pl.ds(0, 7)], p8_out)
@@ -309,10 +349,10 @@
             pltpu.VMEM((2, 384, 256), BF16),
             pltpu.VMEM((128, 512), F32),
             pltpu.VMEM((2, 256, 256), F32),
-            pltpu.VMEM((4, 2, 16, 128), F32),
-            pltpu.VMEM((4, 2, 16, 128), F32),
-            dma((16,)), dma((16,)), dma, dma, dma((3,)), dma((4, 6)), dma, dma((2,)), dma((3,)), dma,
-            dma((7,)), dma, dma((3,)), dma, dma, dma, dma((3,)), dma,
+            pltpu.VMEM((4, 16, 128), F32),
+            pltpu.VMEM((4, 16, 128), F32),
+            dma((16,)), dma((16,)), dma, dma, dma((4,)), dma((4, 6)), dma, dma((2,)), dma((3,)), dma,
+            dma((7,)), dma, dma((3,)), dma, dma, dma, dma((3,)), dma, pltpu.SemaphoreType.REGULAR((3,)),
         ],
         compiler_params=pltpu.CompilerParams(collective_id=0, has_side_effects=True),
     )(

time: 68 us -> 57.2 us (0.84)
  Pallas kernels: 66.6 us -> 55.7 us
    pallas_call x1, Pallas kernels: 66.6 us -> 55.7 us  [local(): pl.pallas_call(kernel, out_shape=jax.ShapeDtypeStruct((16, 8), F32), in_s...]
where the time goes in v2:
time: 57.2 us; the launch traced here: 57 us
  Pallas kernels  55.7 us (97%)
  local copies, waits for them, and re-layouts  1.3 us (2%)
    pallas_call x1, Pallas kernels, local(): pl.pallas_call(kernel, out_shape=jax.ShapeDtypeStruct((16, 8), F32), in_s...  55.7 us
    unnamed x1, local copies, waits for them, and re-layouts  1.3 us

profile of v2, /device:TPU:1, one launch (start us, length us, event | category | flops | bytes accessed | tf_op | source)
XLA Modules:
  0.0 57.0 jit_solution(3588333303471252825)
XLA Ops:
  0.0 55.7 %shard_map.46 = f32[16,8]{1,0:T(8,128)} custom-call(f32[64,16384]{1,0:T(8,128)} %bitcast.10, f32[64,512]{1,0:T(8,128)} %vec.1, f32[32,4,128]{2,1,0:T(4,128)} %bitcast.11, f32[32,2,128]{2,1,0:T(2,128)} %bitcast.12), custom_call_target="tpu_custom_call" | custom-call | tf_op jit(solution)/shard_map/pallas_call | solution.py:331
  55.7 1.3 %copy.6 = f32[2,8,4,2]{1,3,2,0:T(2,128)} copy(f32[2,8,4,2]{1,3,2,0:T(2,128)} %bitcast.13) | data formatting | bytes 1024

commit v3 on v2

--- a/solution.py
+++ b/solution.py
@@ -20,8 +20,8 @@
 
 def kernel(
     amp, vec, rmap, cmap, out,
-    abuf, vbuf, rbuf, cbuf, acc, part, piece8, piece4, slabs, rwide, rcat, ccat, bcat, gbuf, hbuf, msg, res,
-    a_in, a_rin, a_rout, v_in, z_in, x_in, v_out, map_in, c_in, c_out,
+    abuf, vbuf, rbuf, cbuf, acc, part, piece8, piece4, slabs, rwide, rcat, ccat, bcat, gbuf, gswap, hbuf, msg, res,
+    a_in, a_rin, a_rout, v_in, z_in, b_in, r_in, x_in, v_out, map_in, c_in, c_out,
     p8_in, p8_out, p4_in, p4_out, s_in, s_out, m_in, m_out, word,
 ):
     bond, leg = lax.axis_index("bond"), lax.axis_index("leg")
@@ -84,41 +84,75 @@
     pl.semaphore_wait(barrier, 7)
     tell(word.at[0], rounds[0])
 
-    def x_send(i, k):
-        half, way = ((0, 1), (1, -1), (1, 1), (0, -1))[k]
-        n, rows = block_of(i, 0), pl.ds(half * 32, 32)
-        src = vbuf.at[n, rows]
-        return remote(src, vbuf.at[n, rows], v_out, x_in.at[i, k], dev(x_=rot(x, way)))
-
-    def x_relay(i, k):
-        half, way = ((0, 1), (1, -1))[k]
-        n, rows = block_of(i, -way), pl.ds(half * 32, 32)
-        return remote(vbuf.at[n, rows], vbuf.at[n, rows], v_out, x_in.at[i, 4 + k], dev(x_=rot(x, way)))
+    rest = pl.ds(56, 8)
+
+    def rows(half):
+        return (pl.ds(0, 32), pl.ds(32, 24))[half]
+
+    def side(k):
+        return pl.ds(k * 256, 256)
+
+    kinds = ((0, 1), (1, -1), (1, 1), (0, -1))
+
+    def x_send(i, half, k):
+        ref = vbuf.at[block_of(i, 0), rows(half), side(kinds[k][0])]
+        return remote(ref, ref, v_out, x_in.at[i, half, k], dev(x_=rot(x, kinds[k][1])))
+
+    def x_relay(i, half, k):
+        ref = vbuf.at[block_of(i, -kinds[k][1]), rows(half), side(kinds[k][0])]
+        return remote(ref, ref, v_out, x_in.at[i, half, 4 + k], dev(x_=rot(x, kinds[k][1])))
+
+    def r_send(k):
+        return remote(vec.at[rest], vbuf.at[own, rest], v_out, r_in.at[k], dev(x_=rot(x, kinds[k][1])))
+
+    def r_relay(k):
+        ref = vbuf.at[zl * 4 + rot(x, -kinds[k][1]), rest, side(k)]
+        return remote(ref, ref, v_out, r_in.at[2 + k], dev(x_=rot(x, kinds[k][1])))
 
     middle = jnp.logical_and(zl > 0, zl < 3)
 
-    def z_send(i):
-        return remote(vec, vbuf.at[own], v_out, z_in.at[zl], dev(zl_=row_of(i)))
-
-    def z_take(i):
+    def b_copy(r, to):
+        ref = vbuf.at[pl.ds(r * 4, 4), rest]
+        return remote(ref, ref, v_out, b_in.at[r], dev(zl_=to))
+
+    def b_take(i):
         r = row_of(i)
-        n = r * 4 + x
-        remote(vec, vbuf.at[n], v_out, z_in.at[r], dev()).wait_recv()
+        copy = b_copy(r, jnp.where(r > zl, zl - 1, zl + 1))
+        copy.wait_recv()
 
         @pl.when(middle)
         def _():
-            to = jnp.where(r > zl, zl - 1, zl + 1)
-            remote(vbuf.at[n], vbuf.at[n], v_out, z_in.at[r], dev(zl_=to)).start()
-
-    for half, way, k in ((0, 1, 0), (1, -1, 1), (1, 1, 2), (0, -1, 3)):
-        rows = pl.ds(half * 32, 32)
-        remote(vec.at[rows], vbuf.at[own, rows], v_out, x_in.at[0, k], dev(x_=rot(x, way))).start()
-        if k == 1:
-            z_send(1).start()
-
-            @pl.when(middle)
-            def _():
-                z_send(2).start()
+            copy.start()
+
+
+    def z_send(i, half):
+        return remote(vec.at[rows(half)], vbuf.at[own, rows(half)], v_out, z_in.at[zl, half], dev(zl_=row_of(i)))
+
+    def z_take(i, half):
+        r = row_of(i)
+        ref = vbuf.at[r * 4 + x, rows(half)]
+        copy = remote(ref, ref, v_out, z_in.at[r, half], dev(zl_=jnp.where(r > zl, zl - 1, zl + 1)))
+        copy.wait_recv()
+
+        @pl.when(middle)
+        def _():
+            copy.start()
+
+        for k in range(4):
+            x_send(i, half, k).start()
+
+    for k in (0, 1):
+        r_send(k).start()
+    for half in (0, 1):
+        z_send(1, half).start()
+
+        @pl.when(middle)
+        def _():
+            z_send(2, half).start()
+
+        for k, (sd, way) in enumerate(kinds):
+            at = (rows(half), side(sd))
+            remote(vec.at[at], vbuf.at[(own, *at)], v_out, x_in.at[0, half, k], dev(x_=rot(x, way))).start()
     for m in range(4):
         a_local(block_of(0, m)).start()
         a_remote(block_of(0, m)).start()
@@ -130,9 +164,6 @@
         a_local(n).start()
         a_remote(n).start()
 
-    pl.semaphore_wait(word.at[1], 3)
-    tell(word.at[2], rounds[2])
-
     acc[...] = jnp.zeros_like(acc)
 
     def project(n):
@@ -145,18 +176,27 @@
         )
 
     def relay(i):
-        for k in (0, 1):
-            x_send(i, k).wait_recv()
-            x_relay(i, k).start()
+        for half in (0, 1):
+            for k in (0, 1):
+                x_send(i, half, k).wait_recv()
+                x_relay(i, half, k).start()
+
+    def near(i):
+        project(block_of(i, 0))
+        for k in (2, 3):
+            for half in (0, 1):
+                x_send(i, half, k).wait_recv()
+            project(block_of(i, (-1, 1)[k - 2]))
 
     def far(i):
-        for k in (0, 1):
-            x_relay(i, k).wait_recv()
+        for half in (0, 1):
+            for k in (0, 1):
+                x_relay(i, half, k).wait_recv()
         project(block_of(i, 2))
 
-    relay(0)
-    for copy in map_copies:
-        copy.wait()
+    for k in (0, 1):
+        r_send(k).wait_recv()
+        r_relay(k).start()
     c_sends = [
         remote(cbuf.at[zl], cbuf.at[zl], c_out, c_in.at[d - 1], dev(zl_=rot(zl, d))) for d in (1, 2, 3)
     ]
@@ -181,45 +221,74 @@
                 hi, lo = halves(cbuf[k, :, q, :])
                 ccat[k * 64 + q * 32 : k * 64 + q * 32 + 32] = jnp.concatenate([hi, lo, hi], 1)
 
-    @pl.loop(0, 4)
+    pltpu.make_async_copy(vec, vbuf.at[own], v_in).wait()
+
+    @pl.loop(1, 4)
     def _(i):
-        @pl.when(i < 3)
-        def _():
-            @pl.when(jnp.logical_or(i == 0, jnp.logical_not(middle)))
+        edge = jnp.logical_not(middle)
+
+        @pl.when(jnp.logical_or(i == 1, edge))
+        def _():
+            for half in (0, 1):
+                z_take(i, half)
+
+        @pl.when(jnp.logical_and(i < 3, middle))
+        def _():
+            for half in (0, 1):
+                z_take(i + 1, half)
+
+        @pl.when(i == 1)
+        def _():
+            relay(0)
+            for k in (0, 1):
+                r_relay(k).wait_recv()
+            b_copy(zl, row_of(1)).start()
+
+            @pl.when(middle)
             def _():
-                z_take(i + 1)
-
-            for k in range(4):
-                x_send(i + 1, k).start()
-
-        @pl.when(jnp.logical_and(i < 2, middle))
-        def _():
-            z_take(i + 2)
+                b_copy(zl, row_of(2)).start()
+
+            near(0)
+
+        @pl.when(i > 1)
+        def _():
+            relay(i - 1)
+
+        @pl.when(jnp.logical_or(i == 2, jnp.logical_and(i == 3, edge)))
+        def _():
+            b_take(i - 1)
+
+        @pl.when(jnp.logical_and(i > 1, middle))
+        def _():
+            b_take(i)
+
+        @pl.when(jnp.logical_and(i == 3, middle))
+        def _():
+            relay(3)
 
         @pl.when(i == 2)
         def _():
-            for copy in c_sends:
-                copy.start()
-
-        @pl.when(i > 0)
-        def _():
-            relay(i)
-
-        @pl.when(i == 0)
-        def _():
-            pltpu.make_async_copy(vec, vbuf.at[own], v_in).wait()
-
-        project(block_of(i, 0))
-
-        @pl.when(i > 0)
-        def _():
-            far(i - 1)
-
-        x_send(i, 2).wait_recv()
-        project(block_of(i, -1))
-        x_send(i, 3).wait_recv()
-        project(block_of(i, 1))
-
+            far(0)
+            pl.semaphore_wait(word.at[1], 3)
+            tell(word.at[2], rounds[2])
+
+        @pl.when(i == 3)
+        def _():
+            near(1)
+            near(2)
+
+    @pl.when(jnp.logical_not(middle))
+    def _():
+        relay(3)
+        b_take(3)
+
+    far(1)
+    for copy in map_copies:
+        copy.wait()
+    for copy in c_sends:
+        copy.start()
+    near(3)
+    far(2)
     far(3)
 
     both = acc[:128] + acc[128:]
@@ -272,6 +341,9 @@
     gbuf[...] = lax.dot_general(
         jnp.concatenate([l_hi, l_lo, l_hi], 1), rcat[...], NN, preferred_element_type=F32
     )
+    for p in range(4):
+        cols = slice(p * 128, p * 128 + 128)
+        gswap[:, cols] = pltpu.roll(gbuf[:, cols], 64, 1)
     for t in range(2):
         b_hi, b_lo = halves(slabs[t * 128 + 64 : t * 128 + 128])
         for k, v in enumerate((b_hi, b_hi, b_lo)):
@@ -279,28 +351,43 @@
                 bcat[t, k * 128 + par * 64 : k * 128 + par * 64 + 64, par * 128 : par * 128 + 128] = v
         hbuf[t] = lax.dot_general(ccat[...], bcat[t], NN, preferred_element_type=F32)
 
-    row = lax.broadcasted_iota(jnp.int32, (16, 128), 0)
-    lane = lax.broadcasted_iota(jnp.int32, (16, 128), 1)
-    minus = jnp.logical_and(row < 8, lane >= 64)
+    row = lax.broadcasted_iota(jnp.int32, (8, 128), 0)
+    lane = lax.broadcasted_iota(jnp.int32, (8, 128), 1)
+
+    def rows_of_sums(parts):
+        for shift in (1, 2, 4):
+            even = row % (2 * shift) < shift
+            parts = [
+                jnp.where(even, a, b) + pltpu.roll(jnp.where(even, b, a), shift, 0)
+                for a, b in zip(parts[::2], parts[1::2])
+            ]
+        return parts[0]
 
     @pl.loop(0, 4)
     def _(to):
-        total = jnp.zeros((16, 128), F32)
+        totals = [None, None]
         for t in range(2):
-            sums = [[None] * 2 for _ in range(8)]
-            for q in range(2):
-                rows = pl.ds(pl.multiple_of(to * 64 + q * 32, 32), 32)
-                h = [hbuf[t, rows, par * 128 : par * 128 + 128] for par in range(2)]
+            h = [
+                [
+                    hbuf[t, pl.ds(pl.multiple_of(to * 64 + q * 32 + k * 8, 8), 8), par * 128 : par * 128 + 128]
+                    for par in range(2)
+                    for k in range(4)
+                ]
+                for q in range(2)
+            ]
+            for z, g_ref in enumerate((gbuf, gswap)):
+                parts = []
                 for p in range(4):
-                    g = [gbuf[t * 64 + par * 32 : t * 64 + par * 32 + 32, p * 128 : p * 128 + 128] for par in range(2)]
-                    straight = g[0] * h[0] + g[1] * h[1]
-                    crossed = pltpu.roll(g[0], 64, 1) * h[0] + pltpu.roll(g[1], 64, 1) * h[1]
-                    sums[p][q] = jnp.sum(straight, axis=0, keepdims=True)
-                    sums[4 + p][q] = jnp.sum(crossed, axis=0, keepdims=True)
-            v = jnp.concatenate([v for pair in sums for v in pair], 0)
-            v = jnp.sum(jnp.where(minus, -v, v), axis=1, keepdims=True)
-            total = total + jnp.where(lane == zl * 2 + t, v, 0.0)
-        msg[to] = total
+                    g = [g_ref[t * 64 + k * 8 : t * 64 + k * 8 + 8, p * 128 : p * 128 + 128] for k in range(8)]
+                    for q in range(2):
+                        terms = [a * b for a, b in zip(g, h[q])]
+                        parts.append(functools.reduce(jnp.add, terms))
+                v = rows_of_sums(parts)
+                v = jnp.where(lane < 64, v, -v) if z == 0 else v
+                v = jnp.where(lane == zl * 2 + t, jnp.sum(v, axis=1, keepdims=True), 0.0)
+                totals[z] = v if totals[z] is None else totals[z] + v
+        for z in range(2):
+            msg[to, z * 8 : z * 8 + 8] = totals[z]
 
     def answer(d):
         return remote(msg.at[rot(zl, d)], res.at[zl], m_out, m_in.at[d - 1], dev(zl_=rot(zl, d)))
@@ -312,11 +399,11 @@
         answer(d).wait_recv()
     out[...] = jnp.sum(res[...], axis=0)[:, :8]
 
-    drain(vbuf.at[pl.ds(0, 13)], v_out)
+    drain(vbuf.at[pl.ds(0, 14), pl.ds(0, 56)], v_out)
 
     @pl.when(middle)
     def _():
-        drain(vbuf.at[pl.ds(0, 4)], v_out)
+        drain(vbuf.at[pl.ds(0, 11), pl.ds(0, 32)], v_out)
 
     drain(abuf.at[0], a_rout)
     drain(cbuf.at[pl.ds(0, 3)], c_out)
@@ -348,10 +435,11 @@
             pltpu.VMEM((256, 384), BF16),
             pltpu.VMEM((2, 384, 256), BF16),
             pltpu.VMEM((128, 512), F32),
+            pltpu.VMEM((128, 512), F32),
             pltpu.VMEM((2, 256, 256), F32),
             pltpu.VMEM((4, 16, 128), F32),
             pltpu.VMEM((4, 16, 128), F32),
-            dma((16,)), dma((16,)), dma, dma, dma((4,)), dma((4, 6)), dma, dma((2,)), dma((3,)), dma,
+            dma((16,)), dma((16,)), dma, dma, dma((4, 2)), dma((4,)), dma((4,)), dma((4, 2, 6)), dma, dma((2,)), dma((3,)), dma,
             dma((7,)), dma, dma((3,)), dma, dma, dma, dma((3,)), dma, pltpu.SemaphoreType.REGULAR((3,)),
         ],
         compiler_params=pltpu.CompilerParams(collective_id=0, has_side_effects=True),

time: 57.2 us -> 56.4 us (0.986)
  Pallas kernels: 55.7 us -> 54.9 us
    pallas_call x1, Pallas kernels: 55.7 us -> 54.9 us  [local(): pl.pallas_call(kernel, out_shape=jax.ShapeDtypeStruct((16, 8), F32), in_s...]
where the time goes in v3:
time: 56.4 us; the launch traced here: 56.2 us
  Pallas kernels  54.9 us (97%)
  local copies, waits for them, and re-layouts  1.3 us (2%)
    pallas_call x1, Pallas kernels, local(): pl.pallas_call(kernel, out_shape=jax.ShapeDtypeStruct((16, 8), F32), in_s...  54.9 us
    unnamed x1, local copies, waits for them, and re-layouts  1.3 us

profile of v3, /device:TPU:1, one launch (start us, length us, event | category | flops | bytes accessed | tf_op | source)
XLA Modules:
  0.0 56.2 jit_solution(14086268946942036713)
XLA Ops:
  0.0 54.9 %shard_map.46 = f32[16,8]{1,0:T(8,128)} custom-call(f32[64,16384]{1,0:T(8,128)} %bitcast.10, f32[64,512]{1,0:T(8,128)} %vec.1, f32[32,4,128]{2,1,0:T(4,128)} %bitcast.11, f32[32,2,128]{2,1,0:T(2,128)} %bitcast.12), custom_call_target="tpu_custom_call" | custom-call | tf_op jit(solution)/shard_map/pallas_call | solution.py:418
  54.9 1.3 %copy.6 = f32[2,8,4,2]{1,3,2,0:T(2,128)} copy(f32[2,8,4,2]{1,3,2,0:T(2,128)} %bitcast.13) | data formatting | bytes 1024

commit v4 on v3

--- a/solution.py
+++ b/solution.py
@@ -21,7 +21,7 @@
 def kernel(
     amp, vec, rmap, cmap, out,
     abuf, vbuf, rbuf, cbuf, acc, part, piece8, piece4, slabs, rwide, rcat, ccat, bcat, gbuf, gswap, hbuf, msg, res,
-    a_in, a_rin, a_rout, v_in, z_in, b_in, r_in, x_in, v_out, map_in, c_in, c_out,
+    a_in, a_rin, a_rout, v_in, z_in, b_in, r_in, x_in, v_out, r_out, map_in, c_in, c_out,
     p8_in, p8_out, p4_in, p4_out, s_in, s_out, m_in, m_out, word,
 ):
     bond, leg = lax.axis_index("bond"), lax.axis_index("leg")
@@ -103,27 +103,21 @@
         return remote(ref, ref, v_out, x_in.at[i, half, 4 + k], dev(x_=rot(x, kinds[k][1])))
 
     def r_send(k):
-        return remote(vec.at[rest], vbuf.at[own, rest], v_out, r_in.at[k], dev(x_=rot(x, kinds[k][1])))
+        return remote(vec.at[rest], vbuf.at[own, rest], r_out, r_in.at[k], dev(x_=rot(x, kinds[k][1])))
 
     def r_relay(k):
         ref = vbuf.at[zl * 4 + rot(x, -kinds[k][1]), rest, side(k)]
-        return remote(ref, ref, v_out, r_in.at[2 + k], dev(x_=rot(x, kinds[k][1])))
+        return remote(ref, ref, r_out, r_in.at[2 + k], dev(x_=rot(x, kinds[k][1])))
 
     middle = jnp.logical_and(zl > 0, zl < 3)
 
-    def b_copy(r, to):
-        ref = vbuf.at[pl.ds(r * 4, 4), rest]
-        return remote(ref, ref, v_out, b_in.at[r], dev(zl_=to))
+    def b_send(i):
+        ref = vbuf.at[pl.ds(zl * 4, 4), rest]
+        return remote(ref, ref, r_out, b_in.at[zl], dev(zl_=row_of(i)))
 
     def b_take(i):
-        r = row_of(i)
-        copy = b_copy(r, jnp.where(r > zl, zl - 1, zl + 1))
-        copy.wait_recv()
-
-        @pl.when(middle)
-        def _():
-            copy.start()
-
+        ref = vbuf.at[pl.ds(row_of(i) * 4, 4), rest]
+        remote(ref, ref, r_out, b_in.at[row_of(i)], dev()).wait_recv()
 
     def z_send(i, half):
         return remote(vec.at[rows(half)], vbuf.at[own, rows(half)], v_out, z_in.at[zl, half], dev(zl_=row_of(i)))
@@ -223,70 +217,64 @@
 
     pltpu.make_async_copy(vec, vbuf.at[own], v_in).wait()
 
-    @pl.loop(1, 4)
-    def _(i):
-        edge = jnp.logical_not(middle)
-
-        @pl.when(jnp.logical_or(i == 1, edge))
-        def _():
-            for half in (0, 1):
-                z_take(i, half)
-
-        @pl.when(jnp.logical_and(i < 3, middle))
-        def _():
-            for half in (0, 1):
-                z_take(i + 1, half)
-
-        @pl.when(i == 1)
-        def _():
-            relay(0)
-            for k in (0, 1):
-                r_relay(k).wait_recv()
-            b_copy(zl, row_of(1)).start()
-
-            @pl.when(middle)
-            def _():
-                b_copy(zl, row_of(2)).start()
-
-            near(0)
-
-        @pl.when(i > 1)
-        def _():
-            relay(i - 1)
-
-        @pl.when(jnp.logical_or(i == 2, jnp.logical_and(i == 3, edge)))
-        def _():
-            b_take(i - 1)
-
-        @pl.when(jnp.logical_and(i > 1, middle))
-        def _():
-            b_take(i)
-
-        @pl.when(jnp.logical_and(i == 3, middle))
-        def _():
-            relay(3)
-
-        @pl.when(i == 2)
-        def _():
-            far(0)
-            pl.semaphore_wait(word.at[1], 3)
-            tell(word.at[2], rounds[2])
-
-        @pl.when(i == 3)
-        def _():
-            near(1)
-            near(2)
-
-    @pl.when(jnp.logical_not(middle))
+    edge = jnp.logical_not(middle)
+    next_row = jnp.where(middle, 3, 2)
+
+    z_take(1, 0)
+    z_take(1, 1)
+
+    @pl.when(middle)
+    def _():
+        z_take(2, 0)
+        z_take(2, 1)
+
+    relay(0)
+    z_take(next_row, 0)
+    for k in (0, 1):
+        r_relay(k).wait_recv()
+    z_take(next_row, 1)
+    pl.semaphore_wait(word.at[1], 3)
+    tell(word.at[2], rounds[2])
+    for i in (1, 2, 3):
+        b_send(i).start()
+    relay(1)
+
+    @pl.when(middle)
+    def _():
+        near(0)
+        far(0)
+
+    @pl.when(edge)
+    def _():
+        z_take(3, 0)
+        z_take(3, 1)
+
+    relay(2)
+
+    @pl.when(middle)
     def _():
         relay(3)
-        b_take(3)
-
-    far(1)
+
+    @pl.when(edge)
+    def _():
+        near(0)
+        far(0)
+
+    b_take(1)
+    near(1)
+
+    @pl.when(edge)
+    def _():
+        relay(3)
+
     for copy in map_copies:
         copy.wait()
     for copy in c_sends:
         copy.start()
+    b_take(2)
+    near(2)
+    far(1)
+    b_take(3)
     near(3)
     far(2)
     far(3)
@@ -363,13 +351,12 @@
             ]
         return parts[0]
 
-    @pl.loop(0, 4)
-    def _(to):
+    for to in range(4):
         totals = [None, None]
         for t in range(2):
             h = [
                 [
-                    hbuf[t, pl.ds(pl.multiple_of(to * 64 + q * 32 + k * 8, 8), 8), par * 128 : par * 128 + 128]
+                    hbuf[t, pl.ds(to * 64 + q * 32 + k * 8, 8), par * 128 : par * 128 + 128]
                     for par in range(2)
                     for k in range(4)
                 ]
@@ -399,11 +386,12 @@
         answer(d).wait_recv()
     out[...] = jnp.sum(res[...], axis=0)[:, :8]
 
-    drain(vbuf.at[pl.ds(0, 14), pl.ds(0, 56)], v_out)
+    drain(vbuf.at[pl.ds(0, 13), pl.ds(0, 56)], v_out)
+    drain(vbuf.at[pl.ds(0, 15), pl.ds(0, 8)], r_out)
 
     @pl.when(middle)
     def _():
-        drain(vbuf.at[pl.ds(0, 11), pl.ds(0, 32)], v_out)
+        drain(vbuf.at[pl.ds(0, 4), pl.ds(0, 56)], v_out)
 
     drain(abuf.at[0], a_rout)
     drain(cbuf.at[pl.ds(0, 3)], c_out)
@@ -417,7 +405,7 @@
     dma = pltpu.SemaphoreType.DMA
     got = pl.pallas_call(
         kernel,
-        out_shape=jax.ShapeDtypeStruct((16, 8), F32),
+        out_shape=pltpu.VMEM((16, 8), F32),
         in_specs=[pl.BlockSpec(memory_space=pl.ANY)] * 4,
         out_specs=pl.BlockSpec(memory_space=pltpu.VMEM),
         scratch_shapes=[
@@ -439,7 +427,7 @@
             pltpu.VMEM((2, 256, 256), F32),
             pltpu.VMEM((4, 16, 128), F32),
             pltpu.VMEM((4, 16, 128), F32),
-            dma((16,)), dma((16,)), dma, dma, dma((4, 2)), dma((4,)), dma((4,)), dma((4, 2, 6)), dma, dma((2,)), dma((3,)), dma,
+            dma((16,)), dma((16,)), dma, dma, dma((4, 2)), dma((4,)), dma((4,)), dma((4, 2, 6)), dma, dma, dma((2,)), dma((3,)), dma,
             dma((7,)), dma, dma((3,)), dma, dma, dma, dma((3,)), dma, pltpu.SemaphoreType.REGULAR((3,)),
         ],
         compiler_params=pltpu.CompilerParams(collective_id=0, has_side_effects=True),

time: 56.4 us -> 54.4 us (0.965)
  Pallas kernels: 54.9 us -> 53.7 us
  local copies, waits for them, and re-layouts: 1.3 us -> 0.6 us
    pallas_call x1, Pallas kernels: 54.9 us -> 53.7 us  [local(): pl.pallas_call(kernel, out_shape=pltpu.VMEM((16, 8), F32), in_specs=[pl.B...]
    unnamed x1, local copies, waits for them, and re-layouts: 1.3 us -> 0.6 us
where the time goes in v4:
time: 54.4 us; the launch traced here: 54.3 us
  Pallas kernels  53.7 us (99%)
  local copies, waits for them, and re-layouts  0.6 us (1%)
    pallas_call x1, Pallas kernels, local(): pl.pallas_call(kernel, out_shape=pltpu.VMEM((16, 8), F32), in_specs=[pl.B...  53.7 us

profile of v4, /device:TPU:1, one launch (start us, length us, event | category | flops | bytes accessed | tf_op | source)
XLA Modules:
  0.0 54.3 jit_solution(11602873944177487647)
XLA Ops:
  0.0 53.7 %shard_map.46 = f32[16,8]{1,0:T(8,128)S(1)} custom-call(f32[64,16384]{1,0:T(8,128)} %bitcast.11, f32[64,512]{1,0:T(8,128)} %vec.1, f32[32,4,128]{2,1,0:T(4,128)} %bitcast.12, f32[32,2,128]{2,1,0:T(2,128)} %bitcast.13), custom_call_target="tpu_custom_call" | custom-call | tf_op jit(solution)/shard_map/pallas_call | solution.py:406
  53.7 0.6 %copy.6 = f32[2,8,4,2]{1,3,2,0:T(2,128)} copy(f32[2,8,4,2]{1,3,2,0:T(2,128)S(1)} %bitcast.10) | data formatting | bytes 1024

commit v5 on v4

--- a/solution.py
+++ b/solution.py
@@ -46,7 +46,13 @@
         z_ = lax.rem(zh * 4 + zl + (d + 16), 16)
         return dev(zl_=lax.rem(z_, 4), zh_=z_ // 4)
 
-    beside = [dev(x_=rot(x, d)) for d in (1, -1)] + [dev(y_=rot(y, d)) for d in (1, -1)] + [up(1), up(-1)]
+    middle = jnp.logical_and(zl > 0, zl < 3)
+    edge = jnp.logical_not(middle)
+    first = jnp.logical_or(jnp.logical_and(zl == 3, zh < 3), jnp.logical_and(zl == 0, zh == 0))
+    inward = jnp.where(zl == 3, -1, 1)
+    outside = up(-inward)
+    inside = up(inward)
+    beside = [dev(x_=rot(x, d)) for d in (1, -1)] + [dev(y_=rot(y, d)) for d in (1, -1)]
     partner = dev(core_=1 - core)
     rounds = (beside, [partner, up(2), up(-2)], [dev(y_=rot(y, d)) for d in (1, 2, 3)] + [up(4), up(-4)])
 
@@ -55,7 +61,11 @@
             pl.semaphore_signal(sem, inc=1, device_id=device, device_id_type=MESH)
 
     barrier = pltpu.get_barrier_semaphore()
-    tell(barrier, beside + [partner])
+    tell(barrier, beside[:2] + [inside] + beside[2:] + [partner])
+
+    @pl.when(jnp.logical_or(middle, first))
+    def _():
+        tell(barrier, [outside])
 
     own = zl * 4 + x
     pltpu.make_async_copy(vec, vbuf.at[own], v_in).start()
@@ -81,8 +91,14 @@
         cols = pl.ds(pl.multiple_of((n * 2 + 1 - core) * 512, 512), 512)
         return remote(amp.at[:, cols], abuf.at[core, n], a_rout, a_rin.at[n], dev(core_=1 - core))
 
-    pl.semaphore_wait(barrier, 7)
-    tell(word.at[0], rounds[0])
+    @pl.when(first)
+    def _():
+        pl.semaphore_wait(barrier, 6)
+
+    @pl.when(jnp.logical_not(first))
+    def _():
+        pl.semaphore_wait(barrier, 7)
+
 
     rest = pl.ds(56, 8)
 
@@ -108,8 +124,6 @@
     def r_relay(k):
         ref = vbuf.at[zl * 4 + rot(x, -kinds[k][1]), rest, side(k)]
         return remote(ref, ref, r_out, r_in.at[2 + k], dev(x_=rot(x, kinds[k][1])))
-
-    middle = jnp.logical_and(zl > 0, zl < 3)
 
     def b_send(i):
         ref = vbuf.at[pl.ds(zl * 4, 4), rest]
@@ -147,17 +161,27 @@
         for k, (sd, way) in enumerate(kinds):
             at = (rows(half), side(sd))
             remote(vec.at[at], vbuf.at[(own, *at)], v_out, x_in.at[0, half, k], dev(x_=rot(x, way))).start()
-    for m in range(4):
-        a_local(block_of(0, m)).start()
-        a_remote(block_of(0, m)).start()
+    def setup():
+        tell(word.at[0], rounds[0])
+
+        @pl.when(jnp.logical_not(first))
+        def _():
+            tell(word.at[0], [inside, outside])
+
+        @pl.loop(0, 16)
+        def _(m):
+            n = block_of(m // 4, lax.rem(m, 4))
+            a_local(n).start()
+            a_remote(n).start()
+
+    setup()
     pl.semaphore_wait(word.at[0], 6)
+
+    @pl.when(first)
+    def _():
+        tell(word.at[0], [inside, outside])
+
     tell(word.at[1], rounds[1])
-    @pl.loop(4, 16)
-    def _(m):
-        n = block_of(m // 4, lax.rem(m, 4))
-        a_local(n).start()
-        a_remote(n).start()
-
     acc[...] = jnp.zeros_like(acc)
 
     def project(n):
@@ -217,7 +241,6 @@
 
     pltpu.make_async_copy(vec, vbuf.at[own], v_in).wait()
 
-    edge = jnp.logical_not(middle)
     next_row = jnp.where(middle, 3, 2)
 
     z_take(1, 0)
@@ -235,8 +258,12 @@
     z_take(next_row, 1)
     pl.semaphore_wait(word.at[1], 3)
     tell(word.at[2], rounds[2])
-    for i in (1, 2, 3):
-        b_send(i).start()
+
+    def bundles():
+        for i in (1, 2, 3):
+            b_send(i).start()
+
+    pl.when(core == 0)(bundles)
     relay(1)
 
     @pl.when(middle)
@@ -250,6 +277,7 @@
         z_take(3, 1)
 
     relay(2)
+    pl.when(core == 1)(bundles)
 
     @pl.when(middle)
     def _():

time: 54.4 us -> 53.8 us (0.989)
  Pallas kernels: 53.7 us -> 53.1 us
    pallas_call x1, Pallas kernels: 53.7 us -> 53.1 us  [local(): pl.pallas_call(kernel, out_shape=pltpu.VMEM((16, 8), F32), in_specs=[pl.B...]
where the time goes in v5:
time: 53.8 us; the launch traced here: 53.7 us
  Pallas kernels  53.1 us (99%)
  local copies, waits for them, and re-layouts  0.6 us (1%)
    pallas_call x1, Pallas kernels, local(): pl.pallas_call(kernel, out_shape=pltpu.VMEM((16, 8), F32), in_specs=[pl.B...  53.1 us

profile of v5, /device:TPU:1, one launch (start us, length us, event | category | flops | bytes accessed | tf_op | source)
XLA Modules:
  0.0 53.7 jit_solution(8815670791065718512)
XLA Ops:
  0.0 53.1 %shard_map.46 = f32[16,8]{1,0:T(8,128)S(1)} custom-call(f32[64,16384]{1,0:T(8,128)} %bitcast.11, f32[64,512]{1,0:T(8,128)} %vec.1, f32[32,4,128]{2,1,0:T(4,128)} %bitcast.12, f32[32,2,128]{2,1,0:T(2,128)} %bitcast.13), custom_call_target="tpu_custom_call" | custom-call | tf_op jit(solution)/shard_map/pallas_call | solution.py:434
  53.1 0.6 %copy.6 = f32[2,8,4,2]{1,3,2,0:T(2,128)} copy(f32[2,8,4,2]{1,3,2,0:T(2,128)S(1)} %bitcast.10) | data formatting | bytes 1024

commit v6 on v5

--- a/solution.py
+++ b/solution.py
@@ -85,11 +85,11 @@
 
     def a_local(n):
         cols = pl.ds(pl.multiple_of((n * 2 + core) * 512, 512), 512)
-        return pltpu.make_async_copy(amp.at[:, cols], abuf.at[core, n], a_in.at[n])
+        return pltpu.make_async_copy(amp.at[:, cols], abuf.at[core, n], a_in)
 
     def a_remote(n):
         cols = pl.ds(pl.multiple_of((n * 2 + 1 - core) * 512, 512), 512)
-        return remote(amp.at[:, cols], abuf.at[core, n], a_rout, a_rin.at[n], dev(core_=1 - core))
+        return remote(amp.at[:, cols], abuf.at[core, n], a_rout, a_rin, dev(core_=1 - core))
 
     @pl.when(first)
     def _():
@@ -110,20 +110,23 @@
 
     kinds = ((0, 1), (1, -1), (1, 1), (0, -1))
 
+    def x_sem(i, half, k):
+        return x_in.at[i, half * 2 + k if k < 2 else k + 2]
+
     def x_send(i, half, k):
         ref = vbuf.at[block_of(i, 0), rows(half), side(kinds[k][0])]
-        return remote(ref, ref, v_out, x_in.at[i, half, k], dev(x_=rot(x, kinds[k][1])))
+        return remote(ref, ref, v_out, x_sem(i, half, k), dev(x_=rot(x, kinds[k][1])))
 
     def x_relay(i, half, k):
         ref = vbuf.at[block_of(i, -kinds[k][1]), rows(half), side(kinds[k][0])]
-        return remote(ref, ref, v_out, x_in.at[i, half, 4 + k], dev(x_=rot(x, kinds[k][1])))
+        return remote(ref, ref, v_out, x_in.at[i, 6], dev(x_=rot(x, kinds[k][1])))
 
     def r_send(k):
         return remote(vec.at[rest], vbuf.at[own, rest], r_out, r_in.at[k], dev(x_=rot(x, kinds[k][1])))
 
     def r_relay(k):
         ref = vbuf.at[zl * 4 + rot(x, -kinds[k][1]), rest, side(k)]
-        return remote(ref, ref, r_out, r_in.at[2 + k], dev(x_=rot(x, kinds[k][1])))
+        return remote(ref, ref, r_out, r_in.at[2], dev(x_=rot(x, kinds[k][1])))
 
     def b_send(i):
         ref = vbuf.at[pl.ds(zl * 4, 4), rest]
@@ -160,7 +163,7 @@
 
         for k, (sd, way) in enumerate(kinds):
             at = (rows(half), side(sd))
-            remote(vec.at[at], vbuf.at[(own, *at)], v_out, x_in.at[0, half, k], dev(x_=rot(x, way))).start()
+            remote(vec.at[at], vbuf.at[(own, *at)], v_out, x_sem(0, half, k), dev(x_=rot(x, way))).start()
     def setup():
         tell(word.at[0], rounds[0])
 
@@ -185,8 +188,6 @@
     acc[...] = jnp.zeros_like(acc)
 
     def project(n):
-        a_local(n).wait()
-        a_remote(n).wait_recv()
         a_hi, a_lo = halves(abuf[:, n].reshape(128, 512))
         v_hi, v_lo = halves(vbuf[n])
         acc[...] += lax.dot_general(
@@ -201,22 +202,20 @@
 
     def near(i):
         project(block_of(i, 0))
-        for k in (2, 3):
-            for half in (0, 1):
-                x_send(i, half, k).wait_recv()
-            project(block_of(i, (-1, 1)[k - 2]))
+        for k, n in ((2, block_of(i, -1)), (3, block_of(i, 1))):
+            drain(vbuf.at[n, pl.ds(0, 56), side(kinds[k][0])], x_sem(i, 0, k))
+            project(n)
 
     def far(i):
-        for half in (0, 1):
-            for k in (0, 1):
-                x_relay(i, half, k).wait_recv()
-        project(block_of(i, 2))
+        n = block_of(i, 2)
+        drain(vbuf.at[n, pl.ds(0, 56)], x_in.at[i, 6])
+        project(n)
 
     for k in (0, 1):
         r_send(k).wait_recv()
         r_relay(k).start()
     c_sends = [
-        remote(cbuf.at[zl], cbuf.at[zl], c_out, c_in.at[d - 1], dev(zl_=rot(zl, d))) for d in (1, 2, 3)
+        remote(cbuf.at[zl], cbuf.at[zl], c_out, c_in, dev(zl_=rot(zl, d))) for d in (1, 2, 3)
     ]
 
     def maps():
@@ -232,8 +231,7 @@
             for k, w in enumerate((hi, hi, lo)):
                 rcat[k * 128 : k * 128 + 128, p * 128 : p * 128 + 128] = w
         bcat[...] = jnp.zeros_like(bcat)
-        for d in (1, 2, 3):
-            c_sends[d - 1].wait_recv()
+        drain(cbuf.at[pl.ds(0, 3)], c_in)
         for k in range(4):
             for q in range(2):
                 hi, lo = halves(cbuf[k, :, q, :])
@@ -253,8 +251,7 @@
 
     relay(0)
     z_take(next_row, 0)
-    for k in (0, 1):
-        r_relay(k).wait_recv()
+    drain(vbuf.at[own, rest], r_in.at[2])
     z_take(next_row, 1)
     pl.semaphore_wait(word.at[1], 3)
     tell(word.at[2], rounds[2])
@@ -265,6 +262,8 @@
 
     pl.when(core == 0)(bundles)
     relay(1)
+    drain(abuf.at[core], a_in)
+    drain(abuf.at[1 - core], a_rin)
 
     @pl.when(middle)
     def _():
@@ -321,23 +320,21 @@
 
     def scatter(k):
         to = lax.rem(mine + k, 8)
-        return remote(part.at[eighth(to)], piece8.at[mine], p8_out, p8_in.at[k - 1], dev(y_=to // 2, core_=lax.rem(to, 2)))
+        return remote(part.at[eighth(to)], piece8.at[mine], p8_out, p8_in, dev(y_=to // 2, core_=lax.rem(to, 2)))
 
     for k in (5, 4, 3, 2, 6, 7, 1):
         scatter(k).start()
     piece8[mine] = part[eighth(mine)]
-    for k in range(1, 8):
-        scatter(k).wait_recv()
+    drain(piece8.at[pl.ds(0, 7)], p8_in)
     piece4[zh] = jnp.sum(piece8[...], axis=0)
 
     def spread(d):
-        return remote(piece4.at[zh], piece4.at[zh], p4_out, p4_in.at[d - 1], dev(zh_=rot(zh, d)))
+        return remote(piece4.at[zh], piece4.at[zh], p4_out, p4_in, dev(zh_=rot(zh, d)))
 
     for d in (2, 1, 3):
         spread(d).start()
     maps()
-    for d in (1, 2, 3):
-        spread(d).wait_recv()
+    drain(piece4.at[pl.ds(0, 3)], p4_in)
     here = pl.ds(pl.multiple_of(x * 64 + mine * 8, 8), 8)
     slabs[here] = jnp.sum(piece4[...], axis=0)
 
@@ -405,13 +402,12 @@
             msg[to, z * 8 : z * 8 + 8] = totals[z]
 
     def answer(d):
-        return remote(msg.at[rot(zl, d)], res.at[zl], m_out, m_in.at[d - 1], dev(zl_=rot(zl, d)))
+        return remote(msg.at[rot(zl, d)], res.at[zl], m_out, m_in, dev(zl_=rot(zl, d)))
 
     for d in (1, 2, 3):
         answer(d).start()
     res[zl] = msg[zl]
-    for d in (1, 2, 3):
-        answer(d).wait_recv()
+    drain(res.at[pl.ds(0, 3)], m_in)
     out[...] = jnp.sum(res[...], axis=0)[:, :8]
 
     drain(vbuf.at[pl.ds(0, 13), pl.ds(0, 56)], v_out)
@@ -455,8 +451,8 @@
             pltpu.VMEM((2, 256, 256), F32),
             pltpu.VMEM((4, 16, 128), F32),
             pltpu.VMEM((4, 16, 128), F32),
-            dma((16,)), dma((16,)), dma, dma, dma((4, 2)), dma((4,)), dma((4,)), dma((4, 2, 6)), dma, dma, dma((2,)), dma((3,)), dma,
-            dma((7,)), dma, dma((3,)), dma, dma, dma, dma((3,)), dma, pltpu.SemaphoreType.REGULAR((3,)),
+            dma, dma, dma, dma, dma((4, 2)), dma((4,)), dma((3,)), dma((4, 7)), dma, dma, dma((2,)), dma, dma,
+            dma, dma, dma, dma, dma, dma, dma, dma, pltpu.SemaphoreType.REGULAR((3,)),
         ],
         compiler_params=pltpu.CompilerParams(collective_id=0, has_side_effects=True),
     )(

time: 53.8 us -> 53.3 us (level)
    pallas_call x1, Pallas kernels: 53.1 us -> 52.6 us  [local(): pl.pallas_call(kernel, out_shape=pltpu.VMEM((16, 8), F32), in_specs=[pl.B...]
where the time goes in v6:
time: 53.3 us; the launch traced here: 53.2 us
  Pallas kernels  52.6 us (99%)
  local copies, waits for them, and re-layouts  0.6 us (1%)
    pallas_call x1, Pallas kernels, local(): pl.pallas_call(kernel, out_shape=pltpu.VMEM((16, 8), F32), in_specs=[pl.B...  52.6 us

profile of v6, /device:TPU:1, one launch (start us, length us, event | category | flops | bytes accessed | tf_op | source)
XLA Modules:
  0.0 53.2 jit_solution(7350167802564207756)
XLA Ops:
  0.0 52.6 %shard_map.46 = f32[16,8]{1,0:T(8,128)S(1)} custom-call(f32[64,16384]{1,0:T(8,128)} %bitcast.11, f32[64,512]{1,0:T(8,128)} %vec.1, f32[32,4,128]{2,1,0:T(4,128)} %bitcast.12, f32[32,2,128]{2,1,0:T(2,128)} %bitcast.13), custom_call_target="tpu_custom_call" | custom-call | tf_op jit(solution)/shard_map/pallas_call | solution.py:430
  52.6 0.6 %copy.6 = f32[2,8,4,2]{1,3,2,0:T(2,128)} copy(f32[2,8,4,2]{1,3,2,0:T(2,128)S(1)} %bitcast.10) | data formatting | bytes 1024

commit v7 on v6

--- a/solution.py
+++ b/solution.py
@@ -21,8 +21,7 @@
 def kernel(
     amp, vec, rmap, cmap, out,
     abuf, vbuf, rbuf, cbuf, acc, part, piece8, piece4, slabs, rwide, rcat, ccat, bcat, gbuf, gswap, hbuf, msg, res,
-    a_in, a_rin, a_rout, v_in, z_in, b_in, r_in, x_in, v_out, r_out, map_in, c_in, c_out,
-    p8_in, p8_out, p4_in, p4_out, s_in, s_out, m_in, m_out, word,
+    a_in, a_rin, v_in, z_in, b_in, r_in, x_in, v_out, map_in, c_in, c_out, p8_in, p4_in, s_in, m_in, word,
 ):
     bond, leg = lax.axis_index("bond"), lax.axis_index("leg")
     core, x, zl = lax.rem(bond, 2), lax.rem(bond // 2, 4), bond // 8
@@ -89,7 +88,7 @@
 
     def a_remote(n):
         cols = pl.ds(pl.multiple_of((n * 2 + 1 - core) * 512, 512), 512)
-        return remote(amp.at[:, cols], abuf.at[core, n], a_rout, a_rin, dev(core_=1 - core))
+        return remote(amp.at[:, cols], abuf.at[core, n], v_out, a_rin, dev(core_=1 - core))
 
     @pl.when(first)
     def _():
@@ -111,7 +110,7 @@
     kinds = ((0, 1), (1, -1), (1, 1), (0, -1))
 
     def x_sem(i, half, k):
-        return x_in.at[i, half * 2 + k if k < 2 else k + 2]
+        return x_in.at[i, half * 2 + k if k < 2 else 4]
 
     def x_send(i, half, k):
         ref = vbuf.at[block_of(i, 0), rows(half), side(kinds[k][0])]
@@ -119,22 +118,22 @@
 
     def x_relay(i, half, k):
         ref = vbuf.at[block_of(i, -kinds[k][1]), rows(half), side(kinds[k][0])]
-        return remote(ref, ref, v_out, x_in.at[i, 6], dev(x_=rot(x, kinds[k][1])))
+        return remote(ref, ref, v_out, x_in.at[i, 5], dev(x_=rot(x, kinds[k][1])))
 
     def r_send(k):
-        return remote(vec.at[rest], vbuf.at[own, rest], r_out, r_in.at[k], dev(x_=rot(x, kinds[k][1])))
+        return remote(vec.at[rest], vbuf.at[own, rest], v_out, r_in.at[k], dev(x_=rot(x, kinds[k][1])))
 
     def r_relay(k):
         ref = vbuf.at[zl * 4 + rot(x, -kinds[k][1]), rest, side(k)]
-        return remote(ref, ref, r_out, r_in.at[2], dev(x_=rot(x, kinds[k][1])))
+        return remote(ref, ref, v_out, r_in.at[2], dev(x_=rot(x, kinds[k][1])))
 
     def b_send(i):
         ref = vbuf.at[pl.ds(zl * 4, 4), rest]
-        return remote(ref, ref, r_out, b_in.at[zl], dev(zl_=row_of(i)))
+        return remote(ref, ref, v_out, b_in.at[zl], dev(zl_=row_of(i)))
 
     def b_take(i):
         ref = vbuf.at[pl.ds(row_of(i) * 4, 4), rest]
-        remote(ref, ref, r_out, b_in.at[row_of(i)], dev()).wait_recv()
+        remote(ref, ref, v_out, b_in.at[row_of(i)], dev()).wait_recv()
 
     def z_send(i, half):
         return remote(vec.at[rows(half)], vbuf.at[own, rows(half)], v_out, z_in.at[zl, half], dev(zl_=row_of(i)))
@@ -202,13 +201,13 @@
 
     def near(i):
         project(block_of(i, 0))
-        for k, n in ((2, block_of(i, -1)), (3, block_of(i, 1))):
-            drain(vbuf.at[n, pl.ds(0, 56), side(kinds[k][0])], x_sem(i, 0, k))
-            project(n)
+        drain(vbuf.at[block_of(i, -1), pl.ds(0, 56)], x_in.at[i, 4])
+        project(block_of(i, -1))
+        project(block_of(i, 1))
 
     def far(i):
         n = block_of(i, 2)
-        drain(vbuf.at[n, pl.ds(0, 56)], x_in.at[i, 6])
+        drain(vbuf.at[n, pl.ds(0, 56)], x_in.at[i, 5])
         project(n)
 
     for k in (0, 1):
@@ -320,7 +319,7 @@
 
     def scatter(k):
         to = lax.rem(mine + k, 8)
-        return remote(part.at[eighth(to)], piece8.at[mine], p8_out, p8_in, dev(y_=to // 2, core_=lax.rem(to, 2)))
+        return remote(part.at[eighth(to)], piece8.at[mine], v_out, p8_in, dev(y_=to // 2, core_=lax.rem(to, 2)))
 
     for k in (5, 4, 3, 2, 6, 7, 1):
         scatter(k).start()
@@ -329,7 +328,7 @@
     piece4[zh] = jnp.sum(piece8[...], axis=0)
 
     def spread(d):
-        return remote(piece4.at[zh], piece4.at[zh], p4_out, p4_in, dev(zh_=rot(zh, d)))
+        return remote(piece4.at[zh], piece4.at[zh], v_out, p4_in, dev(zh_=rot(zh, d)))
 
     for d in (2, 1, 3):
         spread(d).start()
@@ -343,7 +342,7 @@
             for core_ in (1 - core, core):
                 if dx or dy or core_ is not core:
                     to = dev(x_=rot(x, dx), y_=rot(y, dy), core_=core_)
-                    remote(slabs.at[here], slabs.at[here], s_out, s_in, to).start()
+                    remote(slabs.at[here], slabs.at[here], v_out, s_in, to).start()
 
     drain(slabs.at[pl.ds(0, 248)], s_in)
 
@@ -402,7 +401,7 @@
             msg[to, z * 8 : z * 8 + 8] = totals[z]
 
     def answer(d):
-        return remote(msg.at[rot(zl, d)], res.at[zl], m_out, m_in, dev(zl_=rot(zl, d)))
+        return remote(msg.at[rot(zl, d)], res.at[zl], v_out, m_in, dev(zl_=rot(zl, d)))
 
     for d in (1, 2, 3):
         answer(d).start()
@@ -411,18 +410,18 @@
     out[...] = jnp.sum(res[...], axis=0)[:, :8]
 
     drain(vbuf.at[pl.ds(0, 13), pl.ds(0, 56)], v_out)
-    drain(vbuf.at[pl.ds(0, 15), pl.ds(0, 8)], r_out)
+    drain(vbuf.at[pl.ds(0, 15), pl.ds(0, 8)], v_out)
 
     @pl.when(middle)
     def _():
         drain(vbuf.at[pl.ds(0, 4), pl.ds(0, 56)], v_out)
 
-    drain(abuf.at[0], a_rout)
+    drain(abuf.at[0], v_out)
     drain(cbuf.at[pl.ds(0, 3)], c_out)
-    drain(piece8.at[pl.ds(0, 7)], p8_out)
-    drain(piece4.at[pl.ds(0, 3)], p4_out)
-    drain(slabs.at[pl.ds(0, 248)], s_out)
-    drain(res.at[pl.ds(0, 3)], m_out)
+    drain(piece8.at[pl.ds(0, 7)], v_out)
+    drain(piece4.at[pl.ds(0, 3)], v_out)
+    drain(slabs.at[pl.ds(0, 248)], v_out)
+    drain(res.at[pl.ds(0, 3)], v_out)
 
 
 def local(amplitudes, vectors, row_map, col_map):
@@ -451,8 +450,8 @@
             pltpu.VMEM((2, 256, 256), F32),
             pltpu.VMEM((4, 16, 128), F32),
             pltpu.VMEM((4, 16, 128), F32),
-            dma, dma, dma, dma, dma((4, 2)), dma((4,)), dma((3,)), dma((4, 7)), dma, dma, dma((2,)), dma, dma,
-            dma, dma, dma, dma, dma, dma, dma, dma, pltpu.SemaphoreType.REGULAR((3,)),
+            dma, dma, dma, dma((4, 2)), dma((4,)), dma((3,)), dma((4, 6)), dma, dma((2,)), dma, dma,
+            dma, dma, dma, dma, pltpu.SemaphoreType.REGULAR((3,)),
         ],
         compiler_params=pltpu.CompilerParams(collective_id=0, has_side_effects=True),
     )(

time: 53.3 us -> 53.2 us (level)
  no operation moved by 1% of the time
where the time goes in v7:
time: 53.2 us; the launch traced here: 53.1 us
  Pallas kernels  52.5 us (99%)
  local copies, waits for them, and re-layouts  0.6 us (1%)
    pallas_call x1, Pallas kernels, local(): pl.pallas_call(kernel, out_shape=pltpu.VMEM((16, 8), F32), in_specs=[pl.B...  52.5 us

profile of v7, /device:TPU:1, one launch (start us, length us, event | category | flops | bytes accessed | tf_op | source)
XLA Modules:
  0.0 53.1 jit_solution(6074698058311958547)
XLA Ops:
  0.0 52.5 %shard_map.46 = f32[16,8]{1,0:T(8,128)S(1)} custom-call(f32[64,16384]{1,0:T(8,128)} %bitcast.11, f32[64,512]{1,0:T(8,128)} %vec.1, f32[32,4,128]{2,1,0:T(4,128)} %bitcast.12, f32[32,2,128]{2,1,0:T(2,128)} %bitcast.13), custom_call_target="tpu_custom_call" | custom-call | tf_op jit(solution)/shard_map/pallas_call | solution.py:429
  52.5 0.6 %copy.6 = f32[2,8,4,2]{1,3,2,0:T(2,128)} copy(f32[2,8,4,2]{1,3,2,0:T(2,128)S(1)} %bitcast.10) | data formatting | bytes 1024
